TPU v7x, 128 devices: a whole 4x4x4 slice. The times are simulated.
128 devices in a mesh: seq: 32 (over z, x_lo, y), head: 4 (over x_hi, core).
Axes of the slice: x: 4 (x_hi: 2, x_lo: 2; x = x_hi * 2 + x_lo), y: 4, z: 4, core: 2. Of those that a mesh axis runs over, the one named last changes fastest.
Arguments:
- hidden_in: bfloat16 [12, 2048, 1024], P(None, 'seq'), may hold values from -48 to 48
- lengths: int32 [12], replicated, may hold values from 1 to 2048, as said below
- w_qkv: float32 [1024, 3072], P(('seq', 'head')), may hold values from -0.1875 to 0.1875
- w_attn_out: float32 [1024, 1024], P(('seq', 'head')), may hold values from -0.1875 to 0.1875
- w_in: float32 [1024, 4096], P(('seq', 'head')), may hold values from -0.1875 to 0.1875
- w_down: float32 [4096, 1024], P(('seq', 'head')), may hold values from -0.09375 to 0.09375
- ln_gain: float32 [2, 1024], replicated, may hold values from 0.5 to 1.5
- ln_bias: float32 [2, 1024], replicated, may hold values from -1.5 to 1.5
Outputs:
- hidden_out: bfloat16 [12, 2048, 1024], P(None, 'seq', 'head')
- key_cache: bfloat16 [12, 2048, 1024], P(None, 'seq', 'head')
- value_cache: bfloat16 [12, 2048, 1024], P(None, 'seq', 'head')
Inputs may be any that keep to these rules, and one draw needn't show every extreme that they name: `lengths`: the longest prompt has exactly 2048 positions.
All inputs are finite; a program needn't handle non-finite values.
Results may differ from a plain program's by a relative error of at most 0.014.
Values may be sent and summed in bfloat16 or wider, within the bound.
A program may use at most 192 MiB of HBM per device.

v0:
```python
import jax
import jax.numpy as jnp
from jax import lax
from jax.sharding import PartitionSpec as P

D = 1024
HEADS = 16
HEAD_DIM = 64
EPSILON = 1e-05


def layer_norm(row_values, gain_row, shift_row):
    row_sums, squares = lax.psum(
        (jnp.sum(row_values, axis=1), jnp.sum(row_values * row_values, axis=1)), "head"
    )
    average = (row_sums / D)[:, None]
    spread = (squares / D)[:, None] - average * average
    return (row_values - average) * lax.rsqrt(spread + EPSILON) * gain_row + shift_row


def relayout(qkv_stripe, out_stripe, in_stripe, group_count, seq_count):
    gathered = (
        lax.all_gather(qkv_stripe, "seq", axis=0, tiled=True),
        lax.all_gather(out_stripe, "seq", axis=0, tiled=True),
        lax.all_gather(in_stripe, "seq", axis=0, tiled=True),
    )
    exchanged = (
        lax.all_to_all(gathered[0], "head", split_axis=1, concat_axis=0, tiled=True),
        lax.all_to_all(gathered[1], "head", split_axis=1, concat_axis=0, tiled=True),
        lax.all_to_all(gathered[2], "head", split_axis=1, concat_axis=0, tiled=True),
    )
    result = []
    for piece in exchanged:
        columns = piece.shape[2]
        reordered = piece.reshape(group_count, seq_count, -1, columns).transpose(1, 0, 2, 3)
        result.append(reordered.reshape(-1, columns))
    return tuple(result)


def per_device(hidden_in, lengths, w_qkv, w_attn_out, w_in, w_down, ln_gain, ln_bias):
    group_count = lax.axis_size("head")
    seq_count = lax.axis_size("seq")
    head_group = lax.axis_index("head")
    seq_block = lax.axis_index("seq")
    local_rows = w_qkv.shape[0]
    unit_rows = w_down.shape[0]
    group_width = D // group_count
    heads_here = HEADS // group_count
    prompt_count = hidden_in.shape[0]
    local_span = hidden_in.shape[1]
    qkv_stripe = w_qkv.astype(jnp.bfloat16).reshape(local_rows, 3, group_count, group_width)
    qkv_stripe = qkv_stripe.transpose(0, 2, 1, 3).reshape(local_rows, group_count, 3 * group_width)
    out_stripe = w_attn_out.astype(jnp.bfloat16).reshape(local_rows, group_count, group_width)
    in_stripe = w_in.astype(jnp.bfloat16).reshape(local_rows, seq_count, group_count, unit_rows)
    in_stripe = in_stripe.transpose(0, 2, 1, 3).reshape(
        local_rows, group_count, seq_count * unit_rows
    )
    qkv_weight, out_weight, in_weight = relayout(
        qkv_stripe, out_stripe, in_stripe, group_count, seq_count
    )
    token_rows = hidden_in.reshape(prompt_count * local_span, D)
    projected = jnp.dot(token_rows, qkv_weight, preferred_element_type=jnp.float32).astype(
        jnp.bfloat16
    )
    projected = projected.reshape(prompt_count, local_span, 3, heads_here, HEAD_DIM)
    positions = seq_block * local_span + jnp.arange(local_span, dtype=jnp.int32)
    live_mask = positions[None, :] < lengths[:, None]
    zero_value = jnp.zeros((), jnp.bfloat16)
    queries = projected[:, :, 0]
    keys_here = jnp.where(live_mask[:, :, None, None], projected[:, :, 1], zero_value)
    values_here = jnp.where(live_mask[:, :, None, None], projected[:, :, 2], zero_value)
    keys_all, values_all = (
        lax.all_gather(keys_here, "seq", axis=1, tiled=True),
        lax.all_gather(values_here, "seq", axis=1, tiled=True),
    )
    key_live = jnp.arange(keys_all.shape[1], dtype=jnp.int32)[None, :] < lengths[:, None]
    score_scale = HEAD_DIM ** (-0.5)

    def one_prompt(prompt_items):
        query_rows, key_rows, value_rows, live_keys = prompt_items
        scores = (
            jnp.einsum("qhd,khd->hqk", query_rows, key_rows, preferred_element_type=jnp.float32)
            * score_scale
        )
        scores = jnp.where(live_keys[None, None, :], scores, -jnp.inf)
        row_max = jnp.max(scores, axis=-1, keepdims=True)
        exp_terms = jnp.exp(scores - row_max)
        soft_weights = (exp_terms / jnp.sum(exp_terms, axis=-1, keepdims=True)).astype(jnp.bfloat16)
        head_mix = jnp.einsum(
            "hqk,khd->qhd", soft_weights, value_rows, preferred_element_type=jnp.float32
        )
        return head_mix.astype(jnp.bfloat16)

    attended = lax.map(one_prompt, (queries, keys_all, values_all, key_live))
    attended = attended.reshape(prompt_count * local_span, group_width)
    joined = lax.all_gather(attended, "head", axis=1, tiled=True)
    start = head_group * group_width
    own_columns = lax.dynamic_slice_in_dim(token_rows, start, group_width, 1).astype(jnp.float32)
    gain_first = lax.dynamic_slice_in_dim(ln_gain[0], start, group_width, 0)
    shift_first = lax.dynamic_slice_in_dim(ln_bias[0], start, group_width, 0)
    gain_second = lax.dynamic_slice_in_dim(ln_gain[1], start, group_width, 0)
    shift_second = lax.dynamic_slice_in_dim(ln_bias[1], start, group_width, 0)
    attn_sum = jnp.dot(joined, out_weight, preferred_element_type=jnp.float32) + own_columns
    normed = layer_norm(attn_sum, gain_first, shift_first).astype(jnp.bfloat16)
    normed_all = lax.all_gather(normed, "head", axis=1, tiled=True)
    hidden_units = jax.nn.gelu(
        jnp.dot(normed_all, in_weight, preferred_element_type=jnp.float32), approximate=False
    ).astype(jnp.bfloat16)
    down_weight = lax.all_gather(w_down.astype(jnp.bfloat16), "seq", axis=0, tiled=True)
    partial_terms = jnp.dot(hidden_units, down_weight, preferred_element_type=jnp.float32)
    down_part = lax.psum_scatter(
        partial_terms.astype(jnp.bfloat16), "head", scatter_dimension=1, tiled=True
    ).astype(jnp.float32)
    ffn_sum = down_part + normed.astype(jnp.float32)
    hidden_out = layer_norm(ffn_sum, gain_second, shift_second).astype(jnp.bfloat16)
    hidden_out = hidden_out.reshape(prompt_count, local_span, group_width)
    key_cache = keys_here.reshape(prompt_count, local_span, group_width)
    value_cache = values_here.reshape(prompt_count, local_span, group_width)
    return (hidden_out, key_cache, value_cache)


def solution(mesh):
    in_specs = (
        P(None, "seq", None),
        P(),
        P(("seq", "head"), None),
        P(("seq", "head"), None),
        P(("seq", "head"), None),
        P(("seq", "head"), None),
        P(),
        P(),
    )
    out_specs = (P(None, "seq", "head"), P(None, "seq", "head"), P(None, "seq", "head"))
    return jax.shard_map(
        per_device, mesh=mesh, in_specs=in_specs, out_specs=out_specs, check_vma=False
    )
```

profile of v0, /device:TPU:1, one launch (start us, length us, event | category | flops | bytes accessed | tf_op | source)
XLA Modules:
  0.0 1285.0 jit_solution(5143140646698447728)
XLA Ops:
  8.9 136.6 %all-gather.8.cloned.1.call-done = bf16[256,4,768]{2,0,1:T(8,128)(2,1)} async-done(((bf16[8,4,768]{2,0,1:T(8,128)(2,1)}), bf16[256,4,768]{2,0,1:T(8,128)(2,1)}) %all-gather.8.cloned.1.call-update) | async-done | bytes 1572880 | tf_op jit(solution)/shard_map/all_gather | solution.py:23
  145.4 25.0 %all-to-all-start = ((bf16[256,4,768]{2,0,1:T(8,128)(2,1)}), bf16[256,4,768]{2,0,1:T(8,128)(2,1)S(1)}, u32[]{:S(2)}, u32[]{:S(2)}) async-start(bf16[256,4,768]{2,0,1:T(8,128)(2,1)} %all-gather.8.cloned.1.call-done), calls=%async_computation | async-start | bytes 3145728 | tf_op jit(solution)/shard_map/all_to_all | solution.py:28
  170.7 20.5 %all-to-all-done = bf16[256,4,768]{2,0,1:T(8,128)(2,1)S(1)} async-done(((bf16[256,4,768]{2,0,1:T(8,128)(2,1)}), bf16[256,4,768]{2,0,1:T(8,128)(2,1)S(1)}, u32[]{:S(2)}, u32[]{:S(2)}) %all-to-all-start) | async-done | bytes 1572896 | tf_op jit(solution)/shard_map/all_to_all | solution.py:28
  191.4 2.8 convolution_convert_fusion.2
  201.8 275.5 %all-gather.10.cloned.1.call-done = bf16[12,2048,4,64]{3,2,0,1:T(4,128)(2,1)} async-done(((bf16[12,64,4,64]{3,2,0,1:T(4,128)(2,1)}), bf16[12,2048,4,64]{3,2,0,1:T(4,128)(2,1)}) %all-gather.10.cloned.1.call-update) | async-done | bytes 12582928 | tf_op jit(solution)/shard_map/all_gather | solution.py:74
  477.3 35.9 %copy.59 = bf16[12,2048,4,64]{1,3,2,0:T(8,128)(2,1)} copy(bf16[12,2048,4,64]{3,2,0,1:T(4,128)(2,1)} %all-gather.10.cloned.1.call-done) | data formatting | bytes 25165824 | tf_op jit(solution)/shard_map/while | solution.py:94
  513.2 240.0 %all-gather.12.cloned.1.call-done = bf16[12,2048,4,64]{3,2,0,1:T(4,128)(2,1)} async-done(((bf16[12,64,4,64]{3,2,0,1:T(4,128)(2,1)}), bf16[12,2048,4,64]{3,2,0,1:T(4,128)(2,1)}) %all-gather.12.cloned.1.call-update) | async-done | bytes 12582928 | tf_op jit(solution)/shard_map/all_gather | solution.py:73
  753.2 35.9 %copy.60 = bf16[12,2048,4,64]{1,3,2,0:T(8,128)(2,1)} copy(bf16[12,2048,4,64]{3,2,0,1:T(4,128)(2,1)} %all-gather.12.cloned.1.call-done) | data formatting | bytes 25165824 | tf_op jit(solution)/shard_map/while | solution.py:94
  789.1 71.2 %while.10 = (s32[]{:T(128)}, bf16[12,64,4,64]{3,2,1,0:T(4,128)(2,1)S(1)}, bf16[12,2048,4,64]{1,3,2,0:T(8,128)(2,1)}, pred[12,2048]{1,0:T(8,128)(4,1)S(1)}, bf16[...) while((s32[]{:T(128)}, bf16[12,64,4,64]{3,2,1,0:T(4,128)(2,1)S(1)}, ...), condition=%wide.region_3.4_spmd, body=%wide.region_0.3_spmd.sunk | while | flops 137381888 | bytes 6596181 | solution.py:94
  789.1 3.3 fusion.125
  795.1 3.3 fusion.125
  801.0 3.3 fusion.125
  807.0 3.3 fusion.125
  812.9 3.3 fusion.125
  818.8 3.3 fusion.125
  824.8 3.3 fusion.125
  830.7 3.3 fusion.125
  836.6 3.3 fusion.125
  842.5 3.3 fusion.125
  848.5 3.3 fusion.125
  854.4 3.3 fusion.125
  863.6 71.0 %all_gather.28 = bf16[256,4,256]{2,0,1:T(8,128)(2,1)} all-gather(bf16[8,4,256]{2,0,1:T(8,128)(2,1)S(1)} %bitcast.105), channel_id=1, replica_groups=mesh['seq'=32,'head'=4] {'seq'}, dimensions={0}, use_global_device_ids=true | all-gather | bytes 540672 | tf_op jit(solution)/shard_map/all_gather | solution.py:24
  934.6 18.0 %all-to-all-start.1 = ((bf16[256,4,256]{2,0,1:T(8,128)(2,1)}), bf16[256,4,256]{2,0,1:T(8,128)(2,1)S(1)}, u32[]{:S(2)}, u32[]{:S(2)}) async-start(bf16[256,4,256]{2,0,1:T(8,128)(2,1)} %all_gather.28), calls=%async_computation.1 | async-start | bytes 1048576 | tf_op jit(solution)/shard_map/all_to_all | solution.py:29
  952.7 10.4 all-to-all-done.1
  965.3 7.4 all-reduce.1
  973.8 43.7 %all-gather.18.cloned.1.call-done = bf16[256,4,1024]{2,0,1:T(8,128)(2,1)} async-done(((bf16[8,4,1024]{2,0,1:T(8,128)(2,1)}), bf16[256,4,1024]{2,0,1:T(8,128)(2,1)}) %all-gather.18.cloned.1.call-update) | async-done | bytes 2097168 | tf_op jit(solution)/shard_map/all_gather | solution.py:25
  1017.6 54.6 %all_to_all.45 = bf16[256,4,1024]{2,0,1:T(8,128)(2,1)S(1)} all-to-all(bf16[256,4,1024]{2,0,1:T(8,128)(2,1)} %all-gather.18.cloned.1.call-done), channel_id=1, replica_groups=mesh['seq'=32,'head'=4] {'head'}, dimensions={1} | all-to-all | bytes 4194304 | tf_op jit(solution)/shard_map/all_to_all | solution.py:30
  1073.6 100.2 %all-gather.20.cloned.1.call-done = bf16[1024,1024]{1,0:T(8,128)(2,1)} async-done(((bf16[32,1024]{1,0:T(8,128)(2,1)}), bf16[1024,1024]{1,0:T(8,128)(2,1)}) %all-gather.20.cloned.1.call-update) | async-done | bytes 2097168 | tf_op jit(solution)/shard_map/all_gather | solution.py:109
  1173.8 45.7 %all-gather.16.cloned.1.call-done = bf16[768,1024]{1,0:T(8,128)(2,1)} async-done(((bf16[768,256]{1,0:T(8,128)(2,1)}), bf16[768,1024]{1,0:T(8,128)(2,1)}) %all-gather.16.cloned.1.call-update) | async-done | bytes 1572880 | tf_op jit(solution)/shard_map/all_gather | solution.py:105
  1219.6 13.3 %convolution_convert_fusion.1 = bf16[768,1024]{1,0:T(8,128)(2,1)} fusion(bf16[1024,1024]{1,0:T(8,128)(2,1)} %all-gather.20.cloned.1.call-done, bf16[768,1024]{1,0:T(8,128)(2,1)} %all-gather.16.cloned.1.call-done, bf16[1024,1024]{1,0:T(8,128)(2,1)} %bitcast.96), kind=kOutput, calls=%fused_computation.43 | convolution fusion | flops 3273129984 | bytes 7340032 | tf_op jit(solution)/shard_map/dot_general | solution.py:110
  1235.5 31.7 %reduce-scatter.2.cloned.1.call-done = bf16[768,256]{1,0:T(8,128)(2,1)} async-done(((bf16[768,1024]{1,0:T(8,128)(2,1)}), bf16[768,256]{1,0:T(8,128)(2,1)}) %reduce-scatter.2.cloned.1.call-update) | async-done | bytes 393232 | tf_op jit(solution)/shard_map/reduce_scatter | solution.py:111
  1268.6 7.3 all-reduce
  (120 shorter events, 55.4 us)
Async XLA Ops:
  7.2 163.3 %copy-start.8 = (s32[12]{0:T(128)S(1)}, s32[12]{0:T(128)}, u32[]{:S(2)}) copy-start(s32[12]{0:T(128)} %param.11) | copy-start | bytes 148
  7.2 138.3 %all-gather.8.cloned.1.call-start = ((), (), s32[]{:S(2)}) async-start(), calls=%async_computation.4 | async-start | bytes 1622016 | tf_op jit(solution)/shard_map/all_gather | solution.py:23
  145.4 45.8 %all-to-all-start = ((bf16[256,4,768]{2,0,1:T(8,128)(2,1)}), bf16[256,4,768]{2,0,1:T(8,128)(2,1)S(1)}, u32[]{:S(2)}, u32[]{:S(2)}) async-start(bf16[256,4,768]{2,0,1:T(8,128)(2,1)} %all-gather.8.cloned.1.call-done), calls=%async_computation | async-start | bytes 3145728 | tf_op jit(solution)/shard_map/all_to_all | solution.py:28
  170.5 306.8 %all-gather.10.cloned.1.call-start = ((), (), s32[]{:S(2)}) async-start(), calls=%async_computation.5 | async-start | bytes 25952256 | tf_op jit(solution)/shard_map/all_gather | solution.py:74
  197.4 0.9 copy-start
  197.4 4.2 copy-start.2
  200.7 552.5 %all-gather.12.cloned.1.call-start = ((), (), s32[]{:S(2)}) async-start(), calls=%async_computation.6 | async-start | bytes 25952256 | tf_op jit(solution)/shard_map/all_gather | solution.py:73
  201.4 761.7 %all-gather.14.cloned.1.call-start = ((), (), s32[]{:S(2)}) async-start(), calls=%async_computation.7 | async-start | bytes 1966080 | tf_op jit(solution)/shard_map/all_gather | solution.py:96
  789.1 72.5 %copy-start.3 = (f32[8,4096]{1,0:T(8,128)S(1)}, f32[8,4096]{1,0:T(8,128)}, u32[]{:S(2)}) copy-start(f32[8,4096]{1,0:T(8,128)} %param.14) | copy-start | bytes 393220
  789.1 73.8 %copy-start.4 = (f32[32,1024]{1,0:T(8,128)S(1)}, f32[32,1024]{1,0:T(8,128)}, u32[]{:S(2)}) copy-start(f32[32,1024]{1,0:T(8,128)} %param.15) | copy-start | bytes 393220
  860.3 3.3 copy-start.5
  860.3 92.3 %copy-start.6 = (f32[2,1024]{1,0:T(2,128)S(1)}, f32[2,1024]{1,0:T(2,128)}, u32[]{:S(2)}) copy-start(f32[2,1024]{1,0:T(2,128)} %param.16) | copy-start | bytes 24580
  860.3 92.3 %copy-start.7 = (f32[2,1024]{1,0:T(2,128)S(1)}, f32[2,1024]{1,0:T(2,128)}, u32[]{:S(2)}) copy-start(f32[2,1024]{1,0:T(2,128)} %param.17) | copy-start | bytes 24580
  861.6 156.0 %all-gather.18.cloned.1.call-start = ((), (), s32[]{:S(2)}) async-start(), calls=%async_computation.9 | async-start | bytes 2162688 | tf_op jit(solution)/shard_map/all_gather | solution.py:25
  862.8 311.0 %all-gather.20.cloned.1.call-start = ((), (), s32[]{:S(2)}) async-start(), calls=%async_computation.10 | async-start | bytes 2162688 | tf_op jit(solution)/shard_map/all_gather | solution.py:109
  934.6 28.5 %all-to-all-start.1 = ((bf16[256,4,256]{2,0,1:T(8,128)(2,1)}), bf16[256,4,256]{2,0,1:T(8,128)(2,1)S(1)}, u32[]{:S(2)}, u32[]{:S(2)}) async-start(bf16[256,4,256]{2,0,1:T(8,128)(2,1)} %all_gather.28), calls=%async_computation.1 | async-start | bytes 1048576 | tf_op jit(solution)/shard_map/all_to_all | solution.py:29
  952.6 267.0 %all-gather.16.cloned.1.call-start = ((), (), s32[]{:S(2)}) async-start(), calls=%async_computation.8 | async-start | bytes 1966080 | tf_op jit(solution)/shard_map/all_gather | solution.py:105
  973.8 293.4 %reduce-scatter.2.cloned.1.call-start = ((), (), s32[]{:S(2)}) async-start(), calls=%async_computation.11 | async-start | bytes 1966080 | tf_op jit(solution)/shard_map/reduce_scatter | solution.py:111
  1219.6 13.3 %copy-start.1 = (bf16[12,64,1,4,64]{4,3,2,1,0:T(4,128)(2,1)S(1)}, bf16[12,64,1,4,64]{4,3,2,1,0:T(4,128)(2,1)}, u32[]{:S(2)}) copy-start(bf16[12,64,1,4,64]{4,3,2,1,0:T(4,128)(2,1)} %copy-done) | copy-start | bytes 1179652
Sparse Core Ops, SparseCore 0:
  10.2 135.1 all-gather.7
  200.8 276.4 all-gather.9
  478.9 274.2 all-gather.11
  861.7 21.3 all-gather.13
  885.2 132.3 all-gather.17
  1019.7 154.1 all-gather.19
  1176.1 43.4 all-gather.15
  1233.0 34.1 reduce-scatter.1
where the time goes:
time: 1290 us
  waiting for transfers between devices  905 us (70%)
  blocking collectives  140 us (11%)
  matrix products  86.7 us (7%)
  local copies, waits for them, and re-layouts  84.7 us (7%)
  starting transfers between devices  43.3 us (3%)
  between operations  14.4 us (1%)
    all_gather x1, waiting for transfers between devices, per_device(): lax.all_gather(values_here, 'seq', axis=1, tiled=True)  275 us
    all_gather x1, waiting for transfers between devices, per_device(): lax.all_gather(keys_here, 'seq', axis=1, tiled=True)  240 us
    all_gather x1, waiting for transfers between devices, relayout(): lax.all_gather(qkv_stripe, 'seq', axis=0, tiled=True)  137 us
    all_gather x1, waiting for transfers between devices, per_device(): lax.all_gather(w_down.astype(jnp.bfloat16), 'seq', axis=0, tiled=True)  100 us
    while x2, local copies, waits for them, and re-layouts, per_device(): attended = lax.map(one_prompt, (queries, keys_all, values_all, key_live))  71.8 us
    all_gather x1, blocking collectives, relayout(): lax.all_gather(out_stripe, 'seq', axis=0, tiled=True)  71 us
    all_to_all x1, blocking collectives, relayout(): lax.all_to_all(gathered[2], 'head', split_axis=1, concat_axis=0, tiled=True)  54.6 us
    all_gather x1, waiting for transfers between devices, per_device(): normed_all = lax.all_gather(normed, 'head', axis=1, tiled=True)  45.7 us
  transfers between devices with their start and end apart: 10, of which 9 were waited for; matrix products, arithmetic and copies ran while one was open for 4% of the time, Pallas kernels for 0%

commit v1 on v0

--- a/solution.py
+++ b/solution.py
@@ -20,7 +20,12 @@
 
 def relayout(qkv_stripe, out_stripe, in_stripe, group_count, seq_count):
     gathered = (
-        lax.all_gather(qkv_stripe, "seq", axis=0, tiled=True),
+        jnp.concatenate(
+            lax.all_to_all(
+                jnp.stack([qkv_stripe for _ in range(lax.axis_size("seq"))]), "seq", 0, 0
+            ),
+            axis=0,
+        ),
         lax.all_gather(out_stripe, "seq", axis=0, tiled=True),
         lax.all_gather(in_stripe, "seq", axis=0, tiled=True),
     )

time: 1290 us -> 1160 us (0.90)
  waiting for transfers between devices: 905 us -> 765 us
  blocking collectives: 140 us -> 171 us
  starting transfers between devices: 43.3 us -> 25 us
    all_gather x1 -> x0, waiting for transfers between devices: 137 us -> none  [relayout(): lax.all_gather(qkv_stripe, 'seq', axis=0, tiled=True)]
    all_to_all x0 -> x1, blocking collectives: none -> 30.7 us  [relayout(): lax.all_to_all(jnp.stack([qkv_stripe for _ in range(lax.axis_size('seq'))...]
    all_to_all x1, starting transfers between devices: 25 us -> 6.6 us  [relayout(): lax.all_to_all(gathered[0], 'head', split_axis=1, concat_axis=0, tiled=True)]
  transfers between devices with their start and end apart: 10 -> 9, of which waited for: 9 -> 8; matrix products, arithmetic and copies ran while one was open for 4% -> 4% of each run, Pallas kernels for 0% -> 0%
where the time goes in v1:
time: 1160 us
  waiting for transfers between devices  765 us (66%)
  blocking collectives  171 us (15%)
  matrix products  86.5 us (7%)
  local copies, waits for them, and re-layouts  85.5 us (7%)
  starting transfers between devices  25 us (2%)
  between operations  14.4 us (1%)
    all_gather x1, waiting for transfers between devices, per_device(): lax.all_gather(values_here, 'seq', axis=1, tiled=True)  273 us
    all_gather x1, waiting for transfers between devices, per_device(): lax.all_gather(keys_here, 'seq', axis=1, tiled=True)  240 us
    all_gather x1, waiting for transfers between devices, per_device(): lax.all_gather(w_down.astype(jnp.bfloat16), 'seq', axis=0, tiled=True)  100 us
    while x2, local copies, waits for them, and re-layouts, per_device(): attended = lax.map(one_prompt, (queries, keys_all, values_all, key_live))  71.7 us
    all_gather x1, blocking collectives, relayout(): lax.all_gather(out_stripe, 'seq', axis=0, tiled=True)  70.9 us
    all_to_all x1, blocking collectives, relayout(): lax.all_to_all(gathered[2], 'head', split_axis=1, concat_axis=0, tiled=True)  54.4 us
    all_gather x1, waiting for transfers between devices, per_device(): normed_all = lax.all_gather(normed, 'head', axis=1, tiled=True)  45.6 us
    all_gather x1, waiting for transfers between devices, relayout(): lax.all_gather(in_stripe, 'seq', axis=0, tiled=True)  43.8 us
  transfers between devices with their start and end apart: 9, of which 8 were waited for; matrix products, arithmetic and copies ran while one was open for 4% of the time, Pallas kernels for 0%

profile of v1, /device:TPU:1, one launch (start us, length us, event | category | flops | bytes accessed | tf_op | source)
XLA Modules:
  0.0 1158.1 jit_solution(3501247636033793067)
XLA Ops:
  8.4 30.7 %all_to_all.50 = bf16[32,8,4,768]{3,1,2,0:T(8,128)(2,1)S(1)} all-to-all(bf16[32,8,4,768]{3,1,2,0:T(8,128)(2,1)S(1)} %stack.3), channel_id=1, replica_groups=mesh['seq'=32,'head'=4] {'seq'}, dimensions={0} | all-to-all | bytes 3145728 | tf_op jit(solution)/shard_map/all_to_all | solution.py:24
  40.4 6.6 all-to-all-start.1
  47.2 20.5 %all-to-all-done.1 = bf16[256,4,768]{2,0,1:T(8,128)(2,1)S(1)} async-done(((bf16[256,4,768]{2,0,1:T(8,128)(2,1)}), bf16[256,4,768]{2,0,1:T(8,128)(2,1)S(1)}, u32[]{:S(2)}, u32[]{:S(2)}) %all-to-all-start.1) | async-done | bytes 1572896 | tf_op jit(solution)/shard_map/all_to_all | solution.py:33
  67.9 2.8 convolution_convert_fusion.2
  78.3 272.6 %all-gather.7.cloned.1.call-done = bf16[12,2048,4,64]{3,2,0,1:T(4,128)(2,1)} async-done(((bf16[12,64,4,64]{3,2,0,1:T(4,128)(2,1)}), bf16[12,2048,4,64]{3,2,0,1:T(4,128)(2,1)}) %all-gather.7.cloned.1.call-update) | async-done | bytes 12582928 | tf_op jit(solution)/shard_map/all_gather | solution.py:79
  350.9 35.9 %copy.61 = bf16[12,2048,4,64]{1,3,2,0:T(8,128)(2,1)} copy(bf16[12,2048,4,64]{3,2,0,1:T(4,128)(2,1)} %all-gather.7.cloned.1.call-done) | data formatting | bytes 25165824 | tf_op jit(solution)/shard_map/while | solution.py:99
  386.8 240.0 %all-gather.9.cloned.1.call-done = bf16[12,2048,4,64]{3,2,0,1:T(4,128)(2,1)} async-done(((bf16[12,64,4,64]{3,2,0,1:T(4,128)(2,1)}), bf16[12,2048,4,64]{3,2,0,1:T(4,128)(2,1)}) %all-gather.9.cloned.1.call-update) | async-done | bytes 12582928 | tf_op jit(solution)/shard_map/all_gather | solution.py:78
  626.8 35.8 %copy.62 = bf16[12,2048,4,64]{1,3,2,0:T(8,128)(2,1)} copy(bf16[12,2048,4,64]{3,2,0,1:T(4,128)(2,1)} %all-gather.9.cloned.1.call-done) | data formatting | bytes 25165824 | tf_op jit(solution)/shard_map/while | solution.py:99
  662.6 71.0 %while.10 = (s32[]{:T(128)}, bf16[12,64,4,64]{3,2,1,0:T(4,128)(2,1)S(1)}, bf16[12,2048,4,64]{1,3,2,0:T(8,128)(2,1)}, pred[12,2048]{1,0:T(8,128)(4,1)S(1)}, bf16[...) while((s32[]{:T(128)}, bf16[12,64,4,64]{3,2,1,0:T(4,128)(2,1)S(1)}, ...), condition=%wide.region_3.4_spmd, body=%wide.region_0.3_spmd.sunk | while | flops 137381888 | bytes 6596181 | solution.py:99
  662.7 3.3 fusion.125
  668.7 3.3 fusion.125
  674.6 3.3 fusion.125
  680.5 3.3 fusion.125
  686.4 3.3 fusion.125
  692.3 3.3 fusion.125
  698.2 3.3 fusion.125
  704.1 3.3 fusion.125
  710.0 3.3 fusion.125
  715.9 3.3 fusion.125
  721.9 3.3 fusion.125
  727.8 3.3 fusion.125
  736.9 70.9 %all_gather.24 = bf16[256,4,256]{2,0,1:T(8,128)(2,1)} all-gather(bf16[8,4,256]{2,0,1:T(8,128)(2,1)S(1)} %bitcast.108), channel_id=1, replica_groups=mesh['seq'=32,'head'=4] {'seq'}, dimensions={0}, use_global_device_ids=true | all-gather | bytes 540672 | tf_op jit(solution)/shard_map/all_gather | solution.py:29
  807.8 18.2 %all-to-all-start.2 = ((bf16[256,4,256]{2,0,1:T(8,128)(2,1)}), bf16[256,4,256]{2,0,1:T(8,128)(2,1)S(1)}, u32[]{:S(2)}, u32[]{:S(2)}) async-start(bf16[256,4,256]{2,0,1:T(8,128)(2,1)} %all_gather.24), calls=%async_computation.2 | async-start | bytes 1048576 | tf_op jit(solution)/shard_map/all_to_all | solution.py:34
  826.1 10.3 all-to-all-done.2
  838.6 7.5 all-reduce.1
  847.2 43.8 %all-gather.15.cloned.1.call-done = bf16[256,4,1024]{2,0,1:T(8,128)(2,1)} async-done(((bf16[8,4,1024]{2,0,1:T(8,128)(2,1)}), bf16[256,4,1024]{2,0,1:T(8,128)(2,1)}) %all-gather.15.cloned.1.call-update) | async-done | bytes 2097168 | tf_op jit(solution)/shard_map/all_gather | solution.py:30
  891.0 54.4 %all_to_all.51 = bf16[256,4,1024]{2,0,1:T(8,128)(2,1)S(1)} all-to-all(bf16[256,4,1024]{2,0,1:T(8,128)(2,1)} %all-gather.15.cloned.1.call-done), channel_id=1, replica_groups=mesh['seq'=32,'head'=4] {'head'}, dimensions={1} | all-to-all | bytes 4194304 | tf_op jit(solution)/shard_map/all_to_all | solution.py:35
  946.9 100.1 %all-gather.17.cloned.1.call-done = bf16[1024,1024]{1,0:T(8,128)(2,1)} async-done(((bf16[32,1024]{1,0:T(8,128)(2,1)}), bf16[1024,1024]{1,0:T(8,128)(2,1)}) %all-gather.17.cloned.1.call-update) | async-done | bytes 2097168 | tf_op jit(solution)/shard_map/all_gather | solution.py:114
  1047.1 45.6 %all-gather.13.cloned.1.call-done = bf16[768,1024]{1,0:T(8,128)(2,1)} async-done(((bf16[768,256]{1,0:T(8,128)(2,1)}), bf16[768,1024]{1,0:T(8,128)(2,1)}) %all-gather.13.cloned.1.call-update) | async-done | bytes 1572880 | tf_op jit(solution)/shard_map/all_gather | solution.py:110
  1092.6 13.3 %convolution_convert_fusion.1 = bf16[768,1024]{1,0:T(8,128)(2,1)} fusion(bf16[1024,1024]{1,0:T(8,128)(2,1)} %all-gather.17.cloned.1.call-done, bf16[768,1024]{1,0:T(8,128)(2,1)} %all-gather.13.cloned.1.call-done, bf16[1024,1024]{1,0:T(8,128)(2,1)} %bitcast.99), kind=kOutput, calls=%fused_computation.43 | convolution fusion | flops 3273129984 | bytes 7340032 | tf_op jit(solution)/shard_map/dot_general | solution.py:115
  1108.6 31.6 %reduce-scatter.2.cloned.1.call-done = bf16[768,256]{1,0:T(8,128)(2,1)} async-done(((bf16[768,1024]{1,0:T(8,128)(2,1)}), bf16[768,256]{1,0:T(8,128)(2,1)}) %reduce-scatter.2.cloned.1.call-update) | async-done | bytes 393232 | tf_op jit(solution)/shard_map/reduce_scatter | solution.py:116
  1141.7 7.3 all-reduce
  (120 shorter events, 56.1 us)
Async XLA Ops:
  39.1 7.9 copy-start.8
  40.4 27.3 %all-to-all-start.1 = ((bf16[256,4,768]{2,0,1:T(8,128)(2,1)}), bf16[256,4,768]{2,0,1:T(8,128)(2,1)S(1)}, u32[]{:S(2)}, u32[]{:S(2)}) async-start(bf16[256,4,768]{2,0,1:T(8,128)(2,1)} %bitcast.85), calls=%async_computation.1 | async-start | bytes 3145728 | tf_op jit(solution)/shard_map/all_to_all | solution.py:33
  47.0 303.9 %all-gather.7.cloned.1.call-start = ((), (), s32[]{:S(2)}) async-start(), calls=%async_computation.5 | async-start | bytes 25952256 | tf_op jit(solution)/shard_map/all_gather | solution.py:79
  73.8 0.9 copy-start
  73.8 4.2 copy-start.2
  77.2 549.7 %all-gather.9.cloned.1.call-start = ((), (), s32[]{:S(2)}) async-start(), calls=%async_computation.6 | async-start | bytes 25952256 | tf_op jit(solution)/shard_map/all_gather | solution.py:78
  77.9 758.5 %all-gather.11.cloned.1.call-start = ((), (), s32[]{:S(2)}) async-start(), calls=%async_computation.7 | async-start | bytes 1966080 | tf_op jit(solution)/shard_map/all_gather | solution.py:101
  662.6 72.4 %copy-start.3 = (f32[8,4096]{1,0:T(8,128)S(1)}, f32[8,4096]{1,0:T(8,128)}, u32[]{:S(2)}) copy-start(f32[8,4096]{1,0:T(8,128)} %param.14) | copy-start | bytes 393220
  662.6 73.6 %copy-start.4 = (f32[32,1024]{1,0:T(8,128)S(1)}, f32[32,1024]{1,0:T(8,128)}, u32[]{:S(2)}) copy-start(f32[32,1024]{1,0:T(8,128)} %param.15) | copy-start | bytes 393220
  733.6 3.3 copy-start.5
  733.6 92.3 %copy-start.6 = (f32[2,1024]{1,0:T(2,128)S(1)}, f32[2,1024]{1,0:T(2,128)}, u32[]{:S(2)}) copy-start(f32[2,1024]{1,0:T(2,128)} %param.16) | copy-start | bytes 24580
  733.7 92.4 %copy-start.7 = (f32[2,1024]{1,0:T(2,128)S(1)}, f32[2,1024]{1,0:T(2,128)}, u32[]{:S(2)}) copy-start(f32[2,1024]{1,0:T(2,128)} %param.17) | copy-start | bytes 24580
  734.9 156.1 %all-gather.15.cloned.1.call-start = ((), (), s32[]{:S(2)}) async-start(), calls=%async_computation.9 | async-start | bytes 2162688 | tf_op jit(solution)/shard_map/all_gather | solution.py:30
  736.2 310.9 %all-gather.17.cloned.1.call-start = ((), (), s32[]{:S(2)}) async-start(), calls=%async_computation.10 | async-start | bytes 2162688 | tf_op jit(solution)/shard_map/all_gather | solution.py:114
  807.8 28.5 %all-to-all-start.2 = ((bf16[256,4,256]{2,0,1:T(8,128)(2,1)}), bf16[256,4,256]{2,0,1:T(8,128)(2,1)S(1)}, u32[]{:S(2)}, u32[]{:S(2)}) async-start(bf16[256,4,256]{2,0,1:T(8,128)(2,1)} %all_gather.24), calls=%async_computation.2 | async-start | bytes 1048576 | tf_op jit(solution)/shard_map/all_to_all | solution.py:34
  826.0 266.7 %all-gather.13.cloned.1.call-start = ((), (), s32[]{:S(2)}) async-start(), calls=%async_computation.8 | async-start | bytes 1966080 | tf_op jit(solution)/shard_map/all_gather | solution.py:110
  847.1 293.1 %reduce-scatter.2.cloned.1.call-start = ((), (), s32[]{:S(2)}) async-start(), calls=%async_computation.11 | async-start | bytes 1966080 | tf_op jit(solution)/shard_map/reduce_scatter | solution.py:116
  1092.6 13.4 %copy-start.1 = (bf16[12,64,1,4,64]{4,3,2,1,0:T(4,128)(2,1)S(1)}, bf16[12,64,1,4,64]{4,3,2,1,0:T(4,128)(2,1)}, u32[]{:S(2)}) copy-start(bf16[12,64,1,4,64]{4,3,2,1,0:T(4,128)(2,1)} %copy-done) | copy-start | bytes 1179652
Sparse Core Ops, SparseCore 0:
  77.3 273.5 all-gather.6
  352.5 274.2 all-gather.8
  735.0 21.3 all-gather.10
  758.5 132.4 all-gather.14
  893.1 153.9 all-gather.16
  1049.1 43.4 all-gather.12
  1106.1 34.0 reduce-scatter.1
